TPU v7x, 32 devices: a whole 2x2x4 slice. The times are simulated.
32 devices in a mesh: expert: 8 (over z, y), tensor: 4 (over x, core).
Axes of the slice: x: 2, y: 2, z: 4, core: 2. Of those that a mesh axis runs over, the one named last changes fastest.
Arguments:
- tokens: bfloat16 [1024, 7168], P('expert', 'tensor'), may hold values from -6 to 6
- out_grad: bfloat16 [1024, 7168], P('expert', 'tensor'), may hold values from -1.5 to 1.5
- expert_ids: int32 [1024, 2], P('expert'), may hold values from 0 to 7, all different within a row; in each aligned block of 128 rows (0 to 127, 128 to 255, ...) at most 48 rows name the same one
- gate_values: bfloat16 [1024, 2], P('expert'), may hold values from 0.099609375 to 1
- w_gate: bfloat16 [8, 7168, 1024], P('expert', None, 'tensor'), may hold values from -0.0625 to 0.0625
- w_up: bfloat16 [8, 7168, 1024], P('expert', None, 'tensor'), may hold values from -0.0625 to 0.0625
- w_down: bfloat16 [8, 1024, 7168], P('expert', 'tensor'), may hold values from -0.1875 to 0.1875
Outputs:
- d_tokens: bfloat16 [1024, 7168], P('expert', 'tensor')
- d_gates: float32 [1024, 2], P('expert')
Inputs may be any that keep to these rules, and one draw needn't show every extreme that they name: `expert_ids`: each row names 2 different experts. Among the 128 rows held at one index along `expert` (one aligned block) no expert is named by more than 48 rows, and in some such block one expert is named by exactly 48.
All inputs are finite; a program needn't handle non-finite values.
Results may differ from a plain program's by a relative error of at most 0.0049.
Values may be sent and summed in bfloat16 or wider, within the bound.
A program may use at most 128 MiB of HBM per device.

v0:
```python
import jax
import jax.numpy as jnp
from jax import lax
from jax.sharding import PartitionSpec as P


def local(tokens, out_grad, expert_ids, gate_values, w_gate, w_up, w_down):
    n_experts = lax.axis_size("expert")
    tok_rows, quarter = tokens.shape
    top_count = expert_ids.shape[1]
    most_slots = 3 * tok_rows * top_count // (2 * n_experts)
    slot_count = n_experts * most_slots
    flat_ids = expert_ids.reshape(-1)
    onehot = (flat_ids[:, None] == jnp.arange(n_experts, dtype=jnp.int32)[None, :]).astype(
        jnp.int32
    )
    before = jnp.cumsum(onehot, axis=0) - onehot
    rank = jnp.sum(before * onehot, axis=1)
    slot_of = (flat_ids * most_slots + rank).reshape(tok_rows, top_count)
    matches = slot_of[None, :, :] == jnp.arange(slot_count, dtype=jnp.int32)[:, None, None]
    chooser = jnp.any(matches, axis=2).astype(jnp.bfloat16)
    send_x = jnp.dot(chooser, tokens, preferred_element_type=jnp.float32).astype(jnp.bfloat16)
    send_dy = jnp.dot(chooser, out_grad, preferred_element_type=jnp.float32).astype(jnp.bfloat16)
    gate_wide = gate_values.astype(jnp.float32)[None, :, :]
    send_g = jnp.sum(jnp.where(matches, gate_wide, 0.0), axis=(1, 2)).astype(jnp.bfloat16)
    recv_x, recv_dy, recv_g = (
        lax.all_to_all(
            send_x.reshape(n_experts, most_slots, quarter),
            "expert",
            split_axis=0,
            concat_axis=0,
            tiled=True,
        ),
        lax.all_to_all(
            send_dy.reshape(n_experts, most_slots, quarter),
            "expert",
            split_axis=0,
            concat_axis=0,
            tiled=True,
        ),
        lax.all_to_all(
            send_g.reshape(n_experts, most_slots), "expert", split_axis=0, concat_axis=0, tiled=True
        ),
    )
    rows_x = recv_x.reshape(slot_count, quarter)
    rows_dy = recv_dy.reshape(slot_count, quarter)
    gate_mat = w_gate[0]
    up_mat = w_up[0]
    down_mat = w_down[0]
    piece_x = lax.all_gather(rows_x, "tensor", axis=1, tiled=True)
    piece_dy = lax.all_gather(rows_dy, "tensor", axis=1, tiled=True)
    pre_sum = jnp.dot(piece_x, gate_mat, preferred_element_type=jnp.float32)
    up_sum = jnp.dot(piece_x, up_mat, preferred_element_type=jnp.float32)
    grad_sum = lax.dot_general(
        piece_dy, down_mat, (((1,), (1,)), ((), ())), preferred_element_type=jnp.float32
    )
    sigma = jax.nn.sigmoid(pre_sum)
    active = pre_sum * sigma
    partial_grad = jnp.sum(active * up_sum * grad_sum, axis=1)
    weight_g = recv_g.reshape(slot_count).astype(jnp.float32)
    scaled = weight_g[:, None] * grad_sum
    grad_up = (scaled * active).astype(jnp.bfloat16)
    grad_pre = (scaled * up_sum * sigma * (1.0 + pre_sum * (1.0 - sigma))).astype(jnp.bfloat16)
    contrib = lax.dot_general(
        grad_pre, gate_mat, (((1,), (1,)), ((), ())), preferred_element_type=jnp.float32
    )
    contrib = contrib + lax.dot_general(
        grad_up, up_mat, (((1,), (1,)), ((), ())), preferred_element_type=jnp.float32
    )
    slot_grad = lax.psum(partial_grad, "tensor")
    shares = lax.psum_scatter(
        contrib.astype(jnp.bfloat16), "tensor", scatter_dimension=1, tiled=True
    )
    returned = lax.all_to_all(
        shares.reshape(n_experts, most_slots, quarter),
        "expert",
        split_axis=0,
        concat_axis=0,
        tiled=True,
    )
    returned_grad = lax.all_to_all(
        slot_grad.reshape(n_experts, most_slots), "expert", split_axis=0, concat_axis=0, tiled=True
    )
    d_tokens = lax.dot_general(
        chooser,
        returned.reshape(slot_count, quarter),
        (((0,), (0,)), ((), ())),
        preferred_element_type=jnp.float32,
    ).astype(jnp.bfloat16)
    grad_wide = returned_grad.reshape(slot_count)[:, None, None]
    d_gates = jnp.sum(jnp.where(matches, grad_wide, 0.0), axis=0)
    return (d_tokens, d_gates)


def solution(mesh):
    placed = (
        P("expert", "tensor"),
        P("expert", "tensor"),
        P("expert", None),
        P("expert", None),
        P("expert", None, "tensor"),
        P("expert", None, "tensor"),
        P("expert", "tensor", None),
    )
    return jax.shard_map(
        local,
        mesh=mesh,
        in_specs=placed,
        out_specs=(P("expert", "tensor"), P("expert", None)),
        check_vma=False,
    )
```

profile of v0, /device:TPU:0, one launch (start us, length us, event | category | flops | bytes accessed | tf_op | source)
XLA Modules:
  0.0 276.1 jit_solution(810567907580985810)
XLA Ops:
  7.2 0.9 copy.28
  8.1 0.1 eq.42
  8.2 0.1 eq.38
  8.4 0.6 reduce-window.6
  9.0 0.2 slice_reduce_fusion
  9.2 0.1 fusion.16
  9.3 0.1 reduce_sum.39
  9.5 0.7 multiply_add_fusion
  10.3 0.5 convolution_convert_fusion
  10.8 40.6 %all_to_all.30 = bf16[8,48,1792]{2,1,0:T(8,128)(2,1)} all-to-all(bf16[8,48,1792]{2,1,0:T(8,128)(2,1)S(1)} %bitcast.41), channel_id=1, replica_groups=mesh['expert'=8,'tensor'=4] {'expert'}, dimensions={0} | all-to-all | bytes 2752512 | tf_op jit(solution)/shard_map/all_to_all | solution.py:27
  51.5 0.5 convolution_convert_fusion.1
  52.0 36.1 %all_to_all.31 = bf16[8,48,1792]{2,1,0:T(8,128)(2,1)} all-to-all(bf16[8,48,1792]{2,1,0:T(8,128)(2,1)S(1)} %bitcast.42), channel_id=1, replica_groups=mesh['expert'=8,'tensor'=4] {'expert'}, dimensions={0} | all-to-all | bytes 2752512 | tf_op jit(solution)/shard_map/all_to_all | solution.py:34
  88.2 3.7 %all-gather.5.cloned.1.call-done = bf16[384,7168]{1,0:T(8,128)(2,1)} async-done(((bf16[384,1792]{1,0:T(8,128)(2,1)}), bf16[384,7168]{1,0:T(8,128)(2,1)}) %all-gather.5.cloned.1.call-update) | async-done | bytes 5505040 | tf_op jit(solution)/shard_map/all_gather | solution.py:50
  91.9 5.9 %fusion.2 = f32[384,256]{0,1:T(8,128)S(1)} fusion(bf16[384,7168]{1,0:T(8,128)(2,1)} %all-gather.5.cloned.1.call-done, bf16[1,7168,256]{2,1,0:T(8,128)(2,1)} %param.11), kind=kOutput, calls=%fused_computation.3 | convolution fusion | flops 1409286144 | bytes 9568256 | tf_op jit(solution)/shard_map/dot_general | solution.py:52
  97.8 0.4 copy-done.4
  98.2 2.1 fusion.5
  100.4 35.1 %all-gather.3.cloned.1.call-done = bf16[384,7168]{1,0:T(8,128)(2,1)} async-done(((bf16[384,1792]{1,0:T(8,128)(2,1)}), bf16[384,7168]{1,0:T(8,128)(2,1)}) %all-gather.3.cloned.1.call-update) | async-done | bytes 5505040 | tf_op jit(solution)/shard_map/all_gather | solution.py:51
  135.4 5.8 %multiply_reduce_fusion = (f32[384]{0:T(512)S(1)}, f32[384,256]{0,1:T(8,128)S(1)}) fusion(f32[384,256]{0,1:T(8,128)S(1)} %fusion.5, f32[384,256]{0,1:T(8,128)S(1)} %fusion.2, bf16[384,7168]{1,0:T(8,128)(2,1)} %all-gather.3.cloned.1.call-done, bf16[1,256,7168]{2,1,0:T(8,128)(2,1)} %param.13), kind=kOutput, calls=%fused_computation.14 | convolution fusion | flops 1409973888 | bytes 10356224 | tf_op jit(solution)/shard_map/dot_general | solution.py:54
  141.2 0.1 all_to_all.23
  141.3 6.5 %psum.7 = f32[8,1,48]{2,1,0:T(1,128)} all-reduce(f32[8,1,48]{2,1,0:T(1,128)S(1)} %all_to_all.23), channel_id=1, replica_groups=mesh['expert'=8,'tensor'=4] {'tensor'}, use_global_device_ids=true, to_apply=%region_7.8 | all-reduce | flops 384 | bytes 3072 | tf_op jit(solution)/shard_map/psum | solution.py:70
  147.8 5.7 %all-to-all-start.4 = ((f32[8,1,48]{2,1,0:T(1,128)}), f32[8,1,48]{2,1,0:T(1,128)S(1)}, u32[]{:S(2)}, u32[]{:S(2)}) async-start(f32[8,1,48]{2,1,0:T(1,128)} %psum.7), calls=%async_computation.5 | async-start | bytes 8192 | tf_op jit(solution)/shard_map/all_to_all | solution.py:81
  153.5 6.3 %all-to-all-done.4 = f32[8,1,48]{2,1,0:T(1,128)S(1)} async-done(((f32[8,1,48]{2,1,0:T(1,128)}), f32[8,1,48]{2,1,0:T(1,128)S(1)}, u32[]{:S(2)}, u32[]{:S(2)}) %all-to-all-start.4) | async-done | bytes 1568 | tf_op jit(solution)/shard_map/all_to_all | solution.py:81
  159.8 0.5 broadcast.43
  160.3 0.7 reduce.9
  161.1 0.7 select_reduce_fusion
  161.8 0.1 convert_element_type.67
  161.9 8.8 %all_to_all.32 = bf16[8,1,48]{2,1,0:T(2,128)(2,1)S(1)} all-to-all(bf16[8,1,48]{2,1,0:T(2,128)(2,1)S(1)} %convert_element_type.67), channel_id=1, replica_groups=mesh['expert'=8,'tensor'=4] {'expert'}, dimensions={0} | all-to-all | bytes 1536 | tf_op jit(solution)/shard_map/all_to_all | solution.py:41
  170.8 4.0 %fusion = f32[384,7168]{1,0:T(8,128)S(1)} fusion(bf16[1,7168,256]{2,1,0:T(8,128)(2,1)} %param.11, f32[384,256]{0,1:T(8,128)S(1)} %fusion.2, f32[384,256]{0,1:T(8,128)S(1)} %fusion.5, f32[384,256]{0,1:T(8,128)S(1)} %get-tuple-element.5, f32[384]{0:T(512)S(1)} %reshape.84), kind=kOutput, calls=%fused_computation.1 | convolution fusion | flops 1410367488 | bytes 15861248 | tf_op jit(solution)/shard_map/dot_general | solution.py:64
  174.8 4.1 %add_convert_fusion = bf16[384,7168]{1,0:T(8,128)(2,1)} fusion(f32[384,7168]{1,0:T(8,128)S(1)} %fusion, bf16[1,7168,256]{2,1,0:T(8,128)(2,1)S(1)} %copy-done.2, f32[384,256]{0,1:T(8,128)S(1)} %get-tuple-element.5, f32[384]{0:T(512)S(1)} %reshape.84, f32[384,256]{0,1:T(8,128)S(1)} %fusion.2), kind=kOutput, calls=%fused_computation | convolution fusion | flops 1415479296 | bytes 20973056 | tf_op jit(solution)/shard_map/dot_general | solution.py:67
  178.9 50.5 %reduce-scatter.2.cloned.1.call-done = bf16[384,1792]{1,0:T(8,128)(2,1)} async-done(((bf16[384,7168]{1,0:T(8,128)(2,1)}), bf16[384,1792]{1,0:T(8,128)(2,1)}) %reduce-scatter.2.cloned.1.call-update) | async-done | bytes 1376272 | tf_op jit(solution)/shard_map/reduce_scatter | solution.py:71
  229.4 38.9 %all_to_all.33 = bf16[8,48,1792]{2,1,0:T(8,128)(2,1)S(1)} all-to-all(bf16[8,48,1792]{2,1,0:T(8,128)(2,1)} %bitcast.43), channel_id=1, replica_groups=mesh['expert'=8,'tensor'=4] {'expert'}, dimensions={0} | all-to-all | bytes 2752512 | tf_op jit(solution)/shard_map/all_to_all | solution.py:74
  268.3 1.2 convolution_convert_fusion.2
  (26 shorter events, 0.5 us)
Async XLA Ops:
  7.2 3.1 %copy-start = (bf16[128,1792]{1,0:T(8,128)(2,1)S(1)}, bf16[128,1792]{1,0:T(8,128)(2,1)}, u32[]{:S(2)}) copy-start(bf16[128,1792]{1,0:T(8,128)(2,1)} %param.7) | copy-start | bytes 1376260
  7.2 44.3 %copy-start.3 = (bf16[128,1792]{1,0:T(8,128)(2,1)S(1)}, bf16[128,1792]{1,0:T(8,128)(2,1)}, u32[]{:S(2)}) copy-start(bf16[128,1792]{1,0:T(8,128)(2,1)} %param.8) | copy-start | bytes 1376260
  7.2 84.7 %all-gather.5.cloned.1.call-start = ((), (), s32[]{:S(2)}) async-start(), calls=%async_computation.7 | async-start | bytes 6881280 | tf_op jit(solution)/shard_map/all_gather | solution.py:50
  51.4 84.0 %all-gather.3.cloned.1.call-start = ((), (), s32[]{:S(2)}) async-start(), calls=%async_computation.6 | async-start | bytes 6881280 | tf_op jit(solution)/shard_map/all_gather | solution.py:51
  91.9 5.9 %copy-start.1 = (bf16[1,7168,256]{2,1,0:T(8,128)(2,1)S(1)}, bf16[1,7168,256]{2,1,0:T(8,128)(2,1)}, u32[]{:S(2)}) copy-start(bf16[1,7168,256]{2,1,0:T(8,128)(2,1)} %param.12) | copy-start | bytes 11010052
  91.9 6.3 %copy-start.4 = (bf16[384,7168]{1,0:T(8,128)(2,1)S(1)}, bf16[384,7168]{1,0:T(8,128)(2,1)}, u32[]{:S(2)}) copy-start(bf16[384,7168]{1,0:T(8,128)(2,1)} %all-gather.5.cloned.1.call-done) | copy-start | bytes 16515076
  100.3 53.1 %copy-start.5 = (bf16[128,2]{0,1:T(2,128)(2,1)S(1)}, bf16[128,2]{0,1:T(2,128)(2,1)}, u32[]{:S(2)}) copy-start(bf16[128,2]{0,1:T(2,128)(2,1)} %param.10) | copy-start | bytes 1540
  147.8 12.1 %all-to-all-start.4 = ((f32[8,1,48]{2,1,0:T(1,128)}), f32[8,1,48]{2,1,0:T(1,128)S(1)}, u32[]{:S(2)}, u32[]{:S(2)}) async-start(f32[8,1,48]{2,1,0:T(1,128)} %psum.7), calls=%async_computation.5 | async-start | bytes 8192 | tf_op jit(solution)/shard_map/all_to_all | solution.py:81
  153.4 76.0 %reduce-scatter.2.cloned.1.call-start = ((), (), s32[]{:S(2)}) async-start(), calls=%async_computation.8 | async-start | bytes 6881280 | tf_op jit(solution)/shard_map/reduce_scatter | solution.py:71
  170.8 4.0 %copy-start.2 = (bf16[1,7168,256]{2,1,0:T(8,128)(2,1)S(1)}, bf16[1,7168,256]{2,1,0:T(8,128)(2,1)}, u32[]{:S(2)}) copy-start(bf16[1,7168,256]{2,1,0:T(8,128)(2,1)} %param.12) | copy-start | bytes 11010052
Sparse Core Ops, SparseCore 0:
  51.6 40.2 all-gather.4
  93.4 41.9 all-gather.2
  179.0 50.3 reduce-scatter.1
where the time goes:
time: 276 us
  blocking collectives  131 us (47%)
  waiting for transfers between devices  95.7 us (35%)
  matrix products  24.1 us (9%)
  between operations  13.9 us (5%)
  starting transfers between devices  5.8 us (2%)
  other arithmetic  2.86 us (1%)
  local copies, waits for them, and re-layouts  2.84 us (1%)
    reduce_scatter x1, waiting for transfers between devices, local(): lax.psum_scatter(contrib.astype(jnp.bfloat16), 'tensor', scatter_dimensio...  50.5 us
    all_to_all x1, blocking collectives, local(): lax.all_to_all(send_x.reshape(n_experts, most_slots, quarter), 'expert',...  40.6 us
    all_to_all x1, blocking collectives, local(): lax.all_to_all(shares.reshape(n_experts, most_slots, quarter), 'expert',...  38.9 us
    all_to_all x1, blocking collectives, local(): lax.all_to_all(send_dy.reshape(n_experts, most_slots, quarter), 'expert',...  36.1 us
    all_gather x1, waiting for transfers between devices, local(): piece_dy = lax.all_gather(rows_dy, 'tensor', axis=1, tiled=True)  35.1 us
    all_to_all x1, blocking collectives, local(): lax.all_to_all(send_g.reshape(n_experts, most_slots), 'expert', split_axi...  8.82 us
    psum x1, blocking collectives, local(): slot_grad = lax.psum(partial_grad, 'tensor')  6.49 us
    all_to_all x1, waiting for transfers between devices, local(): lax.all_to_all(slot_grad.reshape(n_experts, most_slots), 'expert', split_...  6.32 us
  transfers between devices with their start and end apart: 4, of which 4 were waited for; matrix products, arithmetic and copies ran while one was open for 3% of the time, Pallas kernels for 0%

commit v1 on v0

--- a/solution.py
+++ b/solution.py
@@ -47,8 +47,11 @@
     gate_mat = w_gate[0]
     up_mat = w_up[0]
     down_mat = w_down[0]
-    piece_x = lax.all_gather(rows_x, "tensor", axis=1, tiled=True)
-    piece_dy = lax.all_gather(rows_dy, "tensor", axis=1, tiled=True)
+    piece_x, piece_dy = jnp.split(
+        lax.all_gather(jnp.concatenate([rows_x, rows_dy], axis=0), "tensor", axis=1, tiled=True),
+        [rows_x.shape[0]],
+        axis=0,
+    )
     pre_sum = jnp.dot(piece_x, gate_mat, preferred_element_type=jnp.float32)
     up_sum = jnp.dot(piece_x, up_mat, preferred_element_type=jnp.float32)
     grad_sum = lax.dot_general(

time: 276 us -> 311 us (1.13)
  waiting for transfers between devices: 95.7 us -> 160 us
  blocking collectives: 131 us -> 91.2 us
  starting transfers between devices: 5.8 us -> 13 us
    all_to_all x1 -> x0, blocking collectives: 36.1 us -> none  [local(): lax.all_to_all(send_dy.reshape(n_experts, most_slots, quarter), 'expert',...]
    all_gather x2 -> x1, waiting for transfers between devices: 38.8 us -> 71.7 us  [local(): lax.all_gather(jnp.concatenate([rows_x, rows_dy], axis=0), 'tensor', axis...]
    all_to_all x0 -> x1, waiting for transfers between devices: none -> 31.2 us  [local(): lax.all_to_all(send_dy.reshape(n_experts, most_slots, quarter), 'expert',...]
    all_to_all x0 -> x1, starting transfers between devices: none -> 7.28 us  [local(): lax.all_to_all(send_dy.reshape(n_experts, most_slots, quarter), 'expert',...]
    dot_general x1, matrix products: 5.76 us -> 2.09 us  [local(): lax.dot_general(piece_dy, down_mat, (((1,), (1,)), ((), ())), preferred_e...]
    all_to_all x1, blocking collectives: 40.6 us -> 37 us  [local(): lax.all_to_all(send_x.reshape(n_experts, most_slots, quarter), 'expert',...]
  transfers between devices with their start and end apart: 4 -> 4, of which waited for: 4 -> 4; matrix products, arithmetic and copies ran while one was open for 3% -> 0% of each run, Pallas kernels for 0% -> 0%
where the time goes in v1:
time: 311 us
  waiting for transfers between devices  160 us (51%)
  blocking collectives  91.2 us (29%)
  matrix products  25.3 us (8%)
  between operations  14.2 us (5%)
  starting transfers between devices  13 us (4%)
  other arithmetic  4.66 us (1%)
    all_gather x1, waiting for transfers between devices, local(): lax.all_gather(jnp.concatenate([rows_x, rows_dy], axis=0), 'tensor', axis...  71.7 us
    reduce_scatter x1, waiting for transfers between devices, local(): lax.psum_scatter(contrib.astype(jnp.bfloat16), 'tensor', scatter_dimensio...  50.5 us
    all_to_all x1, blocking collectives, local(): lax.all_to_all(shares.reshape(n_experts, most_slots, quarter), 'expert',...  38.9 us
    all_to_all x1, blocking collectives, local(): lax.all_to_all(send_x.reshape(n_experts, most_slots, quarter), 'expert',...  37 us
    all_to_all x1, waiting for transfers between devices, local(): lax.all_to_all(send_dy.reshape(n_experts, most_slots, quarter), 'expert',...  31.2 us
    all_to_all x1, blocking collectives, local(): lax.all_to_all(send_g.reshape(n_experts, most_slots), 'expert', split_axi...  8.82 us
    all_to_all x1, starting transfers between devices, local(): lax.all_to_all(send_dy.reshape(n_experts, most_slots, quarter), 'expert',...  7.28 us
    psum x1, blocking collectives, local(): slot_grad = lax.psum(partial_grad, 'tensor')  6.5 us
  transfers between devices with their start and end apart: 4, of which 4 were waited for; matrix products, arithmetic and copies ran while one was open for 0% of the time, Pallas kernels for 0%

profile of v1, /device:TPU:0, one launch (start us, length us, event | category | flops | bytes accessed | tf_op | source)
XLA Modules:
  0.0 310.7 jit_solution(4444639944998616836)
XLA Ops:
  7.2 0.8 copy.28
  8.0 0.1 eq.42
  8.2 0.1 eq.38
  8.3 0.6 reduce-window.6
  8.9 0.2 slice_reduce_fusion
  9.2 0.1 fusion.19
  9.2 0.1 reduce_sum.39
  9.5 0.7 multiply_add_fusion
  10.2 1.6 convolution_convert_fusion
  11.8 7.3 %all-to-all-start.2 = ((bf16[8,48,1792]{2,1,0:T(8,128)(2,1)}), bf16[8,48,1792]{2,1,0:T(8,128)(2,1)S(1)}, u32[]{:S(2)}, u32[]{:S(2)}) async-start(bf16[8,48,1792]{2,1,0:T(8,128)(2,1)} %bitcast.4), calls=%async_computation.2 | async-start | bytes 2752512 | tf_op jit(solution)/shard_map/all_to_all | solution.py:34
  19.1 1.5 convolution_convert_fusion.1
  20.7 31.2 %all-to-all-done.2 = bf16[8,48,1792]{2,1,0:T(8,128)(2,1)S(1)} async-done(((bf16[8,48,1792]{2,1,0:T(8,128)(2,1)}), bf16[8,48,1792]{2,1,0:T(8,128)(2,1)S(1)}, u32[]{:S(2)}, u32[]{:S(2)}) %all-to-all-start.2) | async-done | bytes 1376288 | tf_op jit(solution)/shard_map/all_to_all | solution.py:34
  51.9 37.0 %all_to_all.30 = bf16[8,48,1792]{2,1,0:T(8,128)(2,1)S(1)} all-to-all(bf16[8,48,1792]{2,1,0:T(8,128)(2,1)S(1)} %bitcast.36), channel_id=1, replica_groups=mesh['expert'=8,'tensor'=4] {'expert'}, dimensions={0} | all-to-all | bytes 2752512 | tf_op jit(solution)/shard_map/all_to_all | solution.py:27
  88.9 1.8 pad_maximum_fusion
  90.7 71.7 %all-gather.2.cloned.1.call-done = bf16[768,7168]{1,0:T(8,128)(2,1)} async-done(((bf16[768,1792]{1,0:T(8,128)(2,1)}), bf16[768,7168]{1,0:T(8,128)(2,1)}) %all-gather.2.cloned.1.call-update) | async-done | bytes 11010064 | tf_op jit(solution)/shard_map/all_gather | solution.py:51
  162.5 5.9 %fusion.2 = f32[384,256]{0,1:T(8,128)S(1)} fusion(bf16[768,7168]{1,0:T(8,128)(2,1)} %all-gather.2.cloned.1.call-done, bf16[1,7168,256]{2,1,0:T(8,128)(2,1)} %param.11), kind=kOutput, calls=%fused_computation.3 | convolution fusion | flops 1409286144 | bytes 9568256 | tf_op jit(solution)/shard_map/dot_general | solution.py:55
  168.4 4.9 %fusion.4 = f32[384,256]{0,1:T(8,128)S(1)} fusion(bf16[768,7168]{1,0:T(8,128)(2,1)} %all-gather.2.cloned.1.call-done, bf16[1,7168,256]{2,1,0:T(8,128)(2,1)S(1)} %copy-done.1), kind=kOutput, calls=%fused_computation.5 | convolution fusion | flops 1409286144 | bytes 9568256 | tf_op jit(solution)/shard_map/dot_general | solution.py:56
  173.4 2.1 multiply_reduce_fusion
  175.5 0.1 all_to_all.23
  175.6 6.5 %psum.7 = f32[8,1,48]{2,1,0:T(1,128)} all-reduce(f32[8,1,48]{2,1,0:T(1,128)S(1)} %all_to_all.23), channel_id=1, replica_groups=mesh['expert'=8,'tensor'=4] {'tensor'}, use_global_device_ids=true, to_apply=%region_7.8 | all-reduce | flops 384 | bytes 3072 | tf_op jit(solution)/shard_map/psum | solution.py:73
  182.1 5.7 %all-to-all-start.4 = ((f32[8,1,48]{2,1,0:T(1,128)}), f32[8,1,48]{2,1,0:T(1,128)S(1)}, u32[]{:S(2)}, u32[]{:S(2)}) async-start(f32[8,1,48]{2,1,0:T(1,128)} %psum.7), calls=%async_computation.5 | async-start | bytes 8192 | tf_op jit(solution)/shard_map/all_to_all | solution.py:84
  187.8 6.3 %all-to-all-done.4 = f32[8,1,48]{2,1,0:T(1,128)S(1)} async-done(((f32[8,1,48]{2,1,0:T(1,128)}), f32[8,1,48]{2,1,0:T(1,128)S(1)}, u32[]{:S(2)}, u32[]{:S(2)}) %all-to-all-start.4) | async-done | bytes 1568 | tf_op jit(solution)/shard_map/all_to_all | solution.py:84
  194.2 0.5 broadcast.43
  194.7 0.7 reduce.9
  195.4 0.7 select_reduce_fusion
  196.1 0.1 convert_element_type.67
  196.2 8.8 %all_to_all.31 = bf16[8,1,48]{2,1,0:T(2,128)(2,1)S(1)} all-to-all(bf16[8,1,48]{2,1,0:T(2,128)(2,1)S(1)} %convert_element_type.67), channel_id=1, replica_groups=mesh['expert'=8,'tensor'=4] {'expert'}, dimensions={0} | all-to-all | bytes 1536 | tf_op jit(solution)/shard_map/all_to_all | solution.py:41
  205.1 4.0 %fusion.6 = f32[384,7168]{1,0:T(8,128)S(1)} fusion(bf16[1,7168,256]{2,1,0:T(8,128)(2,1)} %param.11, f32[384,256]{0,1:T(8,128)S(1)} %fusion.2, f32[384,256]{0,1:T(8,128)S(1)} %fusion.4, f32[384,256]{0,1:T(8,128)S(1)} %get-tuple-element.5, f32[384]{0:T(512)S(1)} %reshape.84), kind=kOutput, calls=%fused_computation.7 | convolution fusion | flops 1410367488 | bytes 15861248 | tf_op jit(solution)/shard_map/dot_general | solution.py:67
  209.1 4.1 %add_convert_fusion = bf16[384,7168]{1,0:T(8,128)(2,1)} fusion(f32[384,7168]{1,0:T(8,128)S(1)} %fusion.6, bf16[1,7168,256]{2,1,0:T(8,128)(2,1)S(1)} %copy-done.2, f32[384,256]{0,1:T(8,128)S(1)} %get-tuple-element.5, f32[384]{0:T(512)S(1)} %reshape.84, f32[384,256]{0,1:T(8,128)S(1)} %fusion.2), kind=kOutput, calls=%fused_computation | convolution fusion | flops 1415479296 | bytes 20973056 | tf_op jit(solution)/shard_map/dot_general | solution.py:70
  213.2 50.5 %reduce-scatter.2.cloned.1.call-done = bf16[384,1792]{1,0:T(8,128)(2,1)} async-done(((bf16[384,7168]{1,0:T(8,128)(2,1)}), bf16[384,1792]{1,0:T(8,128)(2,1)}) %reduce-scatter.2.cloned.1.call-update) | async-done | bytes 1376272 | tf_op jit(solution)/shard_map/reduce_scatter | solution.py:74
  263.7 38.9 %all_to_all.32 = bf16[8,48,1792]{2,1,0:T(8,128)(2,1)S(1)} all-to-all(bf16[8,48,1792]{2,1,0:T(8,128)(2,1)} %bitcast.39), channel_id=1, replica_groups=mesh['expert'=8,'tensor'=4] {'expert'}, dimensions={0} | all-to-all | bytes 2752512 | tf_op jit(solution)/shard_map/all_to_all | solution.py:77
  302.7 1.2 convolution_convert_fusion.2
  (30 shorter events, 0.5 us)
Async XLA Ops:
  7.2 3.1 copy-start
  11.8 40.1 %all-to-all-start.2 = ((bf16[8,48,1792]{2,1,0:T(8,128)(2,1)}), bf16[8,48,1792]{2,1,0:T(8,128)(2,1)S(1)}, u32[]{:S(2)}, u32[]{:S(2)}) async-start(bf16[8,48,1792]{2,1,0:T(8,128)(2,1)} %bitcast.4), calls=%async_computation.2 | async-start | bytes 2752512 | tf_op jit(solution)/shard_map/all_to_all | solution.py:34
  19.1 143.4 %all-gather.2.cloned.1.call-start = ((), (), s32[]{:S(2)}) async-start(), calls=%async_computation.6 | async-start | bytes 13762560 | tf_op jit(solution)/shard_map/all_gather | solution.py:51
  162.5 5.9 %copy-start.1 = (bf16[1,7168,256]{2,1,0:T(8,128)(2,1)S(1)}, bf16[1,7168,256]{2,1,0:T(8,128)(2,1)}, u32[]{:S(2)}) copy-start(bf16[1,7168,256]{2,1,0:T(8,128)(2,1)} %param.12) | copy-start | bytes 11010052
  162.5 10.9 %slice-start = ((s8[11010048]{0:T(1024)(128)(4,1)}), s8[4194304]{0:T(1024)(128)(4,1)S(1)}, s32[]{:S(2)}) async-start(s8[11010048]{0:T(1024)(128)(4,1)} %bitcast.40), calls=%async_computation.8 | async-start | bytes 8388608
  162.5 10.9 %slice-start.1 = ((s8[11010048]{0:T(1024)(128)(4,1)}), s8[4194304]{0:T(1024)(128)(4,1)S(1)}, s32[]{:S(2)}) async-start(s8[11010048]{0:T(1024)(128)(4,1)} %bitcast.40), calls=%async_computation.9 | async-start | bytes 8388608
  168.4 5.0 %slice-start.2 = ((s8[11010048]{0:T(1024)(128)(4,1)}), s8[2621440]{0:T(1024)(128)(4,1)S(1)}, s32[]{:S(2)}) async-start(s8[11010048]{0:T(1024)(128)(4,1)} %bitcast.40), calls=%async_computation.10 | async-start | bytes 5242880
  168.4 5.0 %copy-start.3 = (bf16[1,256,7168]{2,1,0:T(8,128)(2,1)S(1)}, bf16[1,256,7168]{2,1,0:T(8,128)(2,1)}, u32[]{:S(2)}) copy-start(bf16[1,256,7168]{2,1,0:T(8,128)(2,1)} %param.13) | copy-start | bytes 11010052
  173.4 14.4 %copy-start.4 = (bf16[128,2]{0,1:T(2,128)(2,1)S(1)}, bf16[128,2]{0,1:T(2,128)(2,1)}, u32[]{:S(2)}) copy-start(bf16[128,2]{0,1:T(2,128)(2,1)} %param.10) | copy-start | bytes 1540
  182.1 12.1 %all-to-all-start.4 = ((f32[8,1,48]{2,1,0:T(1,128)}), f32[8,1,48]{2,1,0:T(1,128)S(1)}, u32[]{:S(2)}, u32[]{:S(2)}) async-start(f32[8,1,48]{2,1,0:T(1,128)} %psum.7), calls=%async_computation.5 | async-start | bytes 8192 | tf_op jit(solution)/shard_map/all_to_all | solution.py:84
  187.8 76.0 %reduce-scatter.2.cloned.1.call-start = ((), (), s32[]{:S(2)}) async-start(), calls=%async_computation.7 | async-start | bytes 6881280 | tf_op jit(solution)/shard_map/reduce_scatter | solution.py:74
  205.1 4.0 %copy-start.2 = (bf16[1,7168,256]{2,1,0:T(8,128)(2,1)S(1)}, bf16[1,7168,256]{2,1,0:T(8,128)(2,1)}, u32[]{:S(2)}) copy-start(bf16[1,7168,256]{2,1,0:T(8,128)(2,1)} %param.12) | copy-start | bytes 11010052
Sparse Core Ops, SparseCore 0:
  90.8 71.5 all-gather.1
  213.4 50.3 reduce-scatter.1
